TPU v7x, 512 devices: a whole 4x4x16 slice. The times are simulated.
512 devices in a mesh: factor: 16 (over x_hi, y, core), load: 32 (over z, x_lo).
Axes of the slice: x: 4 (x_hi: 2, x_lo: 2; x = x_hi * 2 + x_lo), y: 4, z: 16, core: 2. Of those that a mesh axis runs over, the one named last changes fastest.
Arguments:
- b_panel: bfloat16 [2048, 8192], P('factor', 'load'), may hold values from -6 to 6
- b_update: bfloat16 [8192, 8192], P('factor', 'load'), may hold values from -6 to 6
- panel_inverse: bfloat16 [2048, 2048], P('factor'), as said below
- update_factor: bfloat16 [8192, 2048], P('factor'), may hold values from -0.125 to 0.125
- update_solution: bfloat16 [8192, 8192], P(('factor', 'load')), may hold values from -3 to 3
- axle_weights: bfloat16 [3072, 8192], P('load'), may hold values from -0.0625 to 0.0625
Outputs:
- update_rhs: bfloat16 [8192, 8192], P('factor', 'load')
- panel_solution: bfloat16 [2048, 8192], P('factor', 'load')
- config_response: float32 [3072, 2048], P('load', 'factor')
Inputs may be any that keep to these rules, and one draw needn't show every extreme that they name: panel_inverse is zero above the diagonal and its diagonal lies between 1 and 2.
All inputs are finite; a program needn't handle non-finite values.
Results may differ from a plain program's by a relative error of at most 0.0052.
Values may be sent and summed in bfloat16 or wider, within the bound.
A program may use at most 64 MiB of HBM per device.

v0:
```python
import jax
import jax.numpy as jnp
from jax import lax
from jax.sharding import PartitionSpec as P


def local(b_panel, b_update, panel_inverse, update_factor, update_solution, axle_weights):
    block = panel_inverse
    forward = jnp.dot(
        block,
        lax.all_gather(b_panel, "factor", axis=0, tiled=True),
        preferred_element_type=jnp.float32,
    ).astype(jnp.bfloat16)
    block = update_factor
    lowered = jnp.dot(
        block,
        lax.all_gather(forward, "factor", axis=0, tiled=True),
        preferred_element_type=jnp.float32,
    )
    update_rhs = (b_update.astype(jnp.float32) - lowered).astype(jnp.bfloat16)
    regrouped = lax.all_to_all(update_solution, "load", split_axis=1, concat_axis=0, tiled=True)
    factor_cols = lax.all_to_all(update_factor, "factor", split_axis=1, concat_axis=0, tiled=True)
    block = factor_cols
    coupled = lax.dot_general(
        block,
        lax.all_gather(regrouped, "factor", axis=0, tiled=True),
        (((0,), (0,)), ((), ())),
        preferred_element_type=jnp.float32,
    )
    reduced = (forward.astype(jnp.float32) - coupled).astype(jnp.bfloat16)
    block = panel_inverse
    panel_solution = lax.psum_scatter(
        lax.dot_general(
            block, reduced, (((0,), (0,)), ((), ())), preferred_element_type=jnp.float32
        ),
        "factor",
        scatter_dimension=0,
        tiled=True,
    ).astype(jnp.bfloat16)
    block = axle_weights
    config_response = lax.dot_general(
        block,
        lax.all_gather(panel_solution, "load", axis=1, tiled=True),
        (((1,), (1,)), ((), ())),
        preferred_element_type=jnp.float32,
    )
    return (update_rhs, panel_solution, config_response)


def solution(mesh):
    in_specs = (
        P("factor", "load"),
        P("factor", "load"),
        P("factor", None),
        P("factor", None),
        P(("factor", "load"), None),
        P("load", None),
    )
    out_specs = (P("factor", "load"), P("factor", "load"), P("load", "factor"))
    return jax.shard_map(local, mesh=mesh, in_specs=in_specs, out_specs=out_specs, check_vma=False)
```

profile of v0, /device:TPU:8, one launch (start us, length us, event | category | flops | bytes accessed | tf_op | source)
XLA Modules:
  0.0 457.9 jit_solution(6282745598450169393)
XLA Ops:
  7.2 0.0 all-gather.5.cloned.1.call-start
  7.2 0.7 all-gather.5.cloned.1.call-update
  7.9 0.0 all-gather.9.cloned.1.call-start
  8.0 1.0 copy.29
  8.9 38.2 %all_to_all.38 = bf16[16,32,256]{2,0,1:T(8,128)(2,1)} all-to-all(bf16[16,32,256]{2,0,1:T(8,128)(2,1)S(1)} %bitcast.33), channel_id=1, replica_groups=mesh['factor'=16,'load'=32] {'load'}, dimensions={1} | all-to-all | bytes 524288 | tf_op jit(solution)/shard_map/all_to_all | solution.py:21
  47.2 0.0 reduce-scatter.2.cloned.1.call-start
  47.2 3.9 copy.22
  51.1 35.7 %all_to_all.39 = bf16[512,16,128]{0,2,1:T(8,128)(2,1)} all-to-all(bf16[512,16,128]{0,2,1:T(8,128)(2,1)} %bitcast.31), channel_id=1, replica_groups=mesh['factor'=16,'load'=32] {'factor'}, dimensions={1} | all-to-all | bytes 4194304 | tf_op jit(solution)/shard_map/all_to_all | solution.py:22
  86.8 4.0 copy.23
  90.8 1.5 convolution_convert_fusion
  92.4 58.4 %all-gather.9.cloned.1.call-done = bf16[8192,256]{1,0:T(8,128)(2,1)} async-done(((bf16[512,256]{1,0:T(8,128)(2,1)}), bf16[8192,256]{1,0:T(8,128)(2,1)}) %all-gather.9.cloned.1.call-update) | async-done | bytes 4194320 | tf_op jit(solution)/shard_map/all_gather | solution.py:26
  150.8 5.9 %convolution_bitcast_fusion = f32[2048,256]{0,1:T(8,128)} fusion(bf16[128,2048]{1,0:T(8,128)(2,1)S(1)} %copy-done.1, bf16[8192,128]{1,0:T(8,128)(2,1)} %bitcast.29, bf16[8192,256]{1,0:T(8,128)(2,1)} %all-gather.9.cloned.1.call-done, bf16[128,256]{1,0:T(8,128)(2,1)S(1)} %convolution_convert_fusion), kind=kOutput, calls=%fused_computation | convolution fusion | flops 671186944 | bytes 8978432 | tf_op jit(solution)/shard_map/dot_general | solution.py:33
  156.7 0.0 all-gather.7.cloned.1.call-start
  156.7 0.5 all-gather.7.cloned.1.call-update
  157.2 0.0 all-gather.11.cloned.1.call-start
  157.3 92.5 %reduce-scatter.2.cloned.1.call-done = f32[128,256]{0,1:T(8,128)} async-done(((f32[2048,256]{0,1:T(8,128)}), f32[128,256]{0,1:T(8,128)}) %reduce-scatter.2.cloned.1.call-update) | async-done | bytes 131088 | tf_op jit(solution)/shard_map/reduce_scatter | solution.py:32
  249.8 1.5 convert_element_type.23
  251.3 0.1 copy.21
  251.5 61.9 %all-gather.7.cloned.1.call-done = bf16[2048,256]{1,0:T(8,128)(2,1)} async-done(((bf16[128,256]{1,0:T(8,128)(2,1)}), bf16[2048,256]{1,0:T(8,128)(2,1)}) %all-gather.7.cloned.1.call-update) | async-done | bytes 1048592 | tf_op jit(solution)/shard_map/all_gather | solution.py:17
  313.4 2.7 fusion.1
  316.0 0.8 copy.25
  316.9 0.7 copy.26
  317.6 131.0 %all-gather.11.cloned.1.call-done = bf16[128,8192]{0,1:T(8,128)(2,1)} async-done(((bf16[128,256]{0,1:T(8,128)(2,1)}), bf16[128,8192]{0,1:T(8,128)(2,1)}) %all-gather.11.cloned.1.call-update) | async-done | bytes 2097168 | tf_op jit(solution)/shard_map/all_gather | solution.py:43
  448.6 2.8 convolution_bitcast_fusion.2
  (14 shorter events, 0.1 us)
Async XLA Ops:
  7.2 441.5 %copy-start = (bf16[96,8192]{1,0:T(8,128)(2,1)S(1)}, bf16[96,8192]{1,0:T(8,128)(2,1)}, u32[]{:S(2)}) copy-start(bf16[96,8192]{1,0:T(8,128)(2,1)} %param.11) | copy-start | bytes 4718596
  7.2 83.6 %all-gather.5.cloned.1.call-start = ((), (), s32[]{:S(2)}) async-start(), calls=%async_computation.3 | async-start | bytes 1114112 | tf_op jit(solution)/shard_map/all_gather | solution.py:11
  7.9 142.8 %all-gather.9.cloned.1.call-start = ((), (), s32[]{:S(2)}) async-start(), calls=%async_computation.5 | async-start | bytes 4456448 | tf_op jit(solution)/shard_map/all_gather | solution.py:26
  47.2 202.6 %reduce-scatter.2.cloned.1.call-start = ((), (), s32[]{:S(2)}) async-start(), calls=%async_computation.6 | async-start | bytes 2228224 | tf_op jit(solution)/shard_map/reduce_scatter | solution.py:32
  86.8 4.0 copy-start.1
  92.3 64.3 %copy-start.2 = (bf16[128,256]{1,0:T(8,128)(2,1)}, bf16[128,256]{1,0:T(8,128)(2,1)S(1)}, u32[]{:S(2)}) copy-start(bf16[128,256]{1,0:T(8,128)(2,1)S(1)} %convolution_convert_fusion) | copy-start | bytes 196612
  156.6 94.7 %copy-start.4 = (bf16[512,256]{1,0:T(8,128)(2,1)S(1)}, bf16[512,256]{1,0:T(8,128)(2,1)}, u32[]{:S(2)}) copy-start(bf16[512,256]{1,0:T(8,128)(2,1)} %param.7) | copy-start | bytes 786436
  156.7 156.7 %all-gather.7.cloned.1.call-start = ((), (), s32[]{:S(2)}) async-start(), calls=%async_computation.4 | async-start | bytes 1114112 | tf_op jit(solution)/shard_map/all_gather | solution.py:17
  157.2 291.4 %all-gather.11.cloned.1.call-start = ((), (), s32[]{:S(2)}) async-start(), calls=%async_computation.7 | async-start | bytes 2162688 | tf_op jit(solution)/shard_map/all_gather | solution.py:43
  251.5 65.4 %copy-start.3 = (bf16[128,256]{0,1:T(8,128)(2,1)S(1)}, bf16[128,256]{0,1:T(8,128)(2,1)}, u32[]{:S(2)}) copy-start(bf16[128,256]{0,1:T(8,128)(2,1)} %convert_element_type.23) | copy-start | bytes 196612
Sparse Core Ops, SparseCore 0:
  11.4 67.5 all-gather.4
  82.3 68.3 all-gather.8
  156.8 92.9 reduce-scatter.1
  254.1 59.2 all-gather.6
  315.5 133.0 all-gather.10
where the time goes:
time: 458 us
  waiting for transfers between devices  345 us (75%)
  blocking collectives  73.9 us (16%)
  between operations  13.8 us (3%)
  matrix products  12.9 us (3%)
  local copies, waits for them, and re-layouts  10.7 us (2%)
    all_gather x1, waiting for transfers between devices, local(): lax.all_gather(panel_solution, 'load', axis=1, tiled=True)  131 us
    reduce_scatter x1, waiting for transfers between devices, local(): lax.psum_scatter(lax.dot_general(block, reduced, (((0,), (0,)), ((), ()))...  92.5 us
    all_gather x1, waiting for transfers between devices, local(): lax.all_gather(forward, 'factor', axis=0, tiled=True)  61.9 us
    all_gather x1, waiting for transfers between devices, local(): lax.all_gather(regrouped, 'factor', axis=0, tiled=True)  58.4 us
    all_to_all x1, blocking collectives, local(): lax.all_to_all(update_solution, 'load', split_axis=1, concat_axis=0, tile...  38.2 us
    all_to_all x1, blocking collectives, local(): lax.all_to_all(update_factor, 'factor', split_axis=1, concat_axis=0, tile...  35.7 us
  transfers between devices with their start and end apart: 5, of which 4 were waited for; matrix products, arithmetic and copies ran while one was open for 4% of the time, Pallas kernels for 0%

commit v1 on v0

--- a/solution.py
+++ b/solution.py
@@ -40,7 +40,10 @@
     block = axle_weights
     config_response = lax.dot_general(
         block,
-        lax.all_gather(panel_solution, "load", axis=1, tiled=True),
+        jnp.concatenate(
+            lax.all_to_all(jnp.stack([panel_solution] * lax.axis_size("load")), "load", 0, 0),
+            axis=1,
+        ),
         (((1,), (1,)), ((), ())),
         preferred_element_type=jnp.float32,
     )

time: 458 us -> 374 us (0.82)
  the two profiles are of different devices: /device:TPU:8 before, /device:TPU:2 now
where the time goes in v1:
time: 374 us; the launch traced here: 373 us
  waiting for transfers between devices  242 us (65%)
  blocking collectives  76.4 us (20%)
  starting transfers between devices  14.1 us (4%)
  between operations  13.8 us (4%)
  matrix products  12.9 us (3%)
  local copies, waits for them, and re-layouts  12.4 us (3%)
    reduce_scatter x1, waiting for transfers between devices, local(): lax.psum_scatter(lax.dot_general(block, reduced, (((0,), (0,)), ((), ()))...  92.4 us
    all_gather x1, waiting for transfers between devices, local(): lax.all_gather(forward, 'factor', axis=0, tiled=True)  62.6 us
    all_gather x1, waiting for transfers between devices, local(): lax.all_gather(regrouped, 'factor', axis=0, tiled=True)  56.2 us
    all_to_all x1, blocking collectives, local(): lax.all_to_all(update_factor, 'factor', split_axis=1, concat_axis=0, tile...  38.3 us
    all_to_all x1, blocking collectives, local(): lax.all_to_all(update_solution, 'load', split_axis=1, concat_axis=0, tile...  38.2 us
    all_to_all x1, waiting for transfers between devices, local(): lax.all_to_all(jnp.stack([panel_solution] * lax.axis_size('load')), 'load...  30.1 us
    all_to_all x1, starting transfers between devices, local(): lax.all_to_all(jnp.stack([panel_solution] * lax.axis_size('load')), 'load...  14 us
  transfers between devices with their start and end apart: 5, of which 4 were waited for; matrix products, arithmetic and copies ran while one was open for 4% of the time, Pallas kernels for 0%

profile of v1, /device:TPU:2, one launch (start us, length us, event | category | flops | bytes accessed | tf_op | source)
XLA Modules:
  0.0 373.1 jit_solution(2086332847864899456)
XLA Ops:
  7.2 0.7 all-gather.4.cloned.1.call-update
  7.9 0.0 all-gather.8.cloned.1.call-start
  8.0 1.0 copy.30
  8.9 38.2 %all_to_all.43 = bf16[16,32,256]{2,0,1:T(8,128)(2,1)} all-to-all(bf16[16,32,256]{2,0,1:T(8,128)(2,1)S(1)} %bitcast.36), channel_id=1, replica_groups=mesh['factor'=16,'load'=32] {'load'}, dimensions={1} | all-to-all | bytes 524288 | tf_op jit(solution)/shard_map/all_to_all | solution.py:21
  47.1 0.0 reduce-scatter.2.cloned.1.call-start
  47.2 3.9 %copy.23 = bf16[512,2048]{0,1:T(8,128)(2,1)} copy(bf16[512,2048]{1,0:T(8,128)(2,1)} %param.9) | data formatting | bytes 4194304 | tf_op args[3]
  51.1 38.3 %all_to_all.44 = bf16[512,16,128]{0,2,1:T(8,128)(2,1)} all-to-all(bf16[512,16,128]{0,2,1:T(8,128)(2,1)} %bitcast.34), channel_id=1, replica_groups=mesh['factor'=16,'load'=32] {'factor'}, dimensions={1} | all-to-all | bytes 4194304 | tf_op jit(solution)/shard_map/all_to_all | solution.py:22
  89.4 4.0 %copy.24 = bf16[16,512,128]{2,1,0:T(8,128)(2,1)} copy(bf16[16,512,128]{1,2,0:T(8,128)(2,1)} %bitcast.33) | data formatting | bytes 4194304 | tf_op jit(solution)/shard_map/all_to_all | solution.py:22
  93.4 1.5 convolution_convert_fusion
  94.9 56.2 %all-gather.8.cloned.1.call-done = bf16[8192,256]{1,0:T(8,128)(2,1)} async-done(((bf16[512,256]{1,0:T(8,128)(2,1)}), bf16[8192,256]{1,0:T(8,128)(2,1)}) %all-gather.8.cloned.1.call-update) | async-done | bytes 4194320 | tf_op jit(solution)/shard_map/all_gather | solution.py:26
  151.1 5.9 %convolution_bitcast_fusion = f32[2048,256]{0,1:T(8,128)} fusion(bf16[128,2048]{1,0:T(8,128)(2,1)S(1)} %copy-done.1, bf16[8192,128]{1,0:T(8,128)(2,1)} %bitcast.32, bf16[8192,256]{1,0:T(8,128)(2,1)} %all-gather.8.cloned.1.call-done, bf16[128,256]{1,0:T(8,128)(2,1)S(1)} %convolution_convert_fusion), kind=kOutput, calls=%fused_computation | convolution fusion | flops 671186944 | bytes 8978432 | tf_op jit(solution)/shard_map/dot_general | solution.py:33
  157.0 92.4 %reduce-scatter.2.cloned.1.call-done = f32[128,256]{0,1:T(8,128)} async-done(((f32[2048,256]{0,1:T(8,128)}), f32[128,256]{0,1:T(8,128)}) %reduce-scatter.2.cloned.1.call-update) | async-done | bytes 131088 | tf_op jit(solution)/shard_map/reduce_scatter | solution.py:32
  249.4 0.9 convert_element_type.23
  250.3 1.8 stack.2
  252.1 14.0 %all-to-all-start.2 = ((bf16[32,128,256]{1,2,0:T(8,128)(2,1)}), bf16[32,128,256]{1,2,0:T(8,128)(2,1)}, u32[]{:S(2)}, u32[]{:S(2)}) async-start(bf16[32,128,256]{1,2,0:T(8,128)(2,1)} %stack.2), calls=%async_computation.3 | async-start | bytes 4194304 | tf_op jit(solution)/shard_map/all_to_all | solution.py:44
  266.1 0.0 all-gather.6.cloned.1.call-start
  266.2 0.5 all-gather.6.cloned.1.call-update
  266.7 0.1 copy.22
  266.8 62.6 %all-gather.6.cloned.1.call-done = bf16[2048,256]{1,0:T(8,128)(2,1)} async-done(((bf16[128,256]{1,0:T(8,128)(2,1)}), bf16[2048,256]{1,0:T(8,128)(2,1)}) %all-gather.6.cloned.1.call-update) | async-done | bytes 1048592 | tf_op jit(solution)/shard_map/all_gather | solution.py:17
  329.4 2.7 fusion.1
  332.1 0.8 copy.26
  332.9 0.7 copy.27
  333.7 30.1 %all-to-all-done.2 = bf16[32,128,256]{1,2,0:T(8,128)(2,1)} async-done(((bf16[32,128,256]{1,2,0:T(8,128)(2,1)}), bf16[32,128,256]{1,2,0:T(8,128)(2,1)}, u32[]{:S(2)}, u32[]{:S(2)}) %all-to-all-start.2) | async-done | bytes 2097184 | tf_op jit(solution)/shard_map/all_to_all | solution.py:44
  363.7 2.8 convolution_bitcast_fusion.2
  (12 shorter events, 0.1 us)
Async XLA Ops:
  7.2 356.6 %copy-start = (bf16[96,8192]{1,0:T(8,128)(2,1)S(1)}, bf16[96,8192]{1,0:T(8,128)(2,1)}, u32[]{:S(2)}) copy-start(bf16[96,8192]{1,0:T(8,128)(2,1)} %param.11) | copy-start | bytes 4718596
  7.2 86.2 %all-gather.4.cloned.1.call-start = ((), (), s32[]{:S(2)}) async-start(), calls=%async_computation.4 | async-start | bytes 1114112 | tf_op jit(solution)/shard_map/all_gather | solution.py:11
  7.9 143.2 %all-gather.8.cloned.1.call-start = ((), (), s32[]{:S(2)}) async-start(), calls=%async_computation.6 | async-start | bytes 4456448 | tf_op jit(solution)/shard_map/all_gather | solution.py:26
  47.1 202.3 %reduce-scatter.2.cloned.1.call-start = ((), (), s32[]{:S(2)}) async-start(), calls=%async_computation.7 | async-start | bytes 2228224 | tf_op jit(solution)/shard_map/reduce_scatter | solution.py:32
  89.4 4.0 %copy-start.1 = (bf16[128,2048]{1,0:T(8,128)(2,1)S(1)}, bf16[128,2048]{1,0:T(8,128)(2,1)}, u32[]{:S(2)}) copy-start(bf16[128,2048]{1,0:T(8,128)(2,1)} %param.8) | copy-start | bytes 1572868
  94.9 62.1 %copy-start.2 = (bf16[128,256]{1,0:T(8,128)(2,1)}, bf16[128,256]{1,0:T(8,128)(2,1)S(1)}, u32[]{:S(2)}) copy-start(bf16[128,256]{1,0:T(8,128)(2,1)S(1)} %convolution_convert_fusion) | copy-start | bytes 196612
  252.1 14.6 %copy-start.3 = (bf16[512,256]{1,0:T(8,128)(2,1)S(1)}, bf16[512,256]{1,0:T(8,128)(2,1)}, u32[]{:S(2)}) copy-start(bf16[512,256]{1,0:T(8,128)(2,1)} %param.7) | copy-start | bytes 786436
  252.1 111.6 %all-to-all-start.2 = ((bf16[32,128,256]{1,2,0:T(8,128)(2,1)}), bf16[32,128,256]{1,2,0:T(8,128)(2,1)}, u32[]{:S(2)}, u32[]{:S(2)}) async-start(bf16[32,128,256]{1,2,0:T(8,128)(2,1)} %stack.2), calls=%async_computation.3 | async-start | bytes 4194304 | tf_op jit(solution)/shard_map/all_to_all | solution.py:44
  266.1 63.3 %all-gather.6.cloned.1.call-start = ((), (), s32[]{:S(2)}) async-start(), calls=%async_computation.5 | async-start | bytes 1114112 | tf_op jit(solution)/shard_map/all_gather | solution.py:17
Sparse Core Ops, SparseCore 0:
  11.4 68.2 all-gather.3
  82.9 68.1 all-gather.7
  157.2 92.1 reduce-scatter.1
  271.1 58.2 all-gather.5
